TPU v7x, 32 devices: a whole 2x2x4 slice. The times are simulated.
32 devices in a mesh: wide: 8 (over y, x, core), blk: 4 (over z).
Axes of the slice: x: 2, y: 2, z: 4, core: 2. Of those that a mesh axis runs over, the one named last changes fastest.
Arguments:
- sources: bfloat16 [32, 64000], P(('wide', 'blk')), may hold values from -6 to 6
- targets: bfloat16 [4, 64000], P('blk'), may hold values from -6 to 6
Outputs:
- exchange_field: float32 [4, 64000], P('blk', 'wide')
All inputs are finite; a program needn't handle non-finite values.
Results may differ from a plain program's by a relative error of at most 0.014.
Values may be sent and summed in bfloat16 or wider, within the bound.
A program may use at most 64 MiB of HBM per device.

v0:
```python
import math

import jax
import jax.numpy as jnp
from jax import lax
from jax.sharding import PartitionSpec as P

GRID = 40
HOPS = 2


screen = 0.3


def from_behind(block, axis, distance):
    devices = range(lax.axis_size(axis))
    route = [((i - distance) % len(devices), i) for i in devices]
    return lax.ppermute(block, axis, route)


def tables(grid):
    index = jnp.arange(grid, dtype=jnp.int32)
    product = index[:, None] * index[None, :] % grid
    angle = 2.0 * math.pi / grid * product.astype(jnp.float32)
    return jnp.concatenate([jnp.cos(angle), jnp.sin(angle)], axis=0).astype(jnp.bfloat16)


def kernel_table(grid):
    index = jnp.arange(grid, dtype=jnp.int32)
    wrapped = (index + grid // 2) % grid - grid // 2
    wave = 2.0 * math.pi / grid * wrapped.astype(jnp.float32)
    square = wave * wave
    total = square[:, None, None] + square[None, :, None] + square[None, None, :]
    values = 4.0 * math.pi / (total + screen * screen) / float(grid**3)
    return values.reshape(grid, grid * grid)


def turn(field, both):
    width = both.shape[1]
    cos_table = both[:width]
    sin_table = both[width:]
    cpart = jnp.einsum("mnr,kn->mrk", field, cos_table, preferred_element_type=jnp.float32)
    spart = jnp.einsum("mnr,kn->mrk", field, sin_table, preferred_element_type=jnp.float32)
    return (cpart.reshape(field.shape), spart.reshape(field.shape))


def potential(pair, both, kern):
    cpart, spart = turn(pair, both)
    real_part = cpart.astype(jnp.bfloat16)
    imag_part = (-spart).astype(jnp.bfloat16)
    for section in range(2):
        rcos, rsin = turn(real_part, both)
        icos, isin = turn(imag_part, both)
        new_real = rcos + isin
        new_imag = icos - rsin
        if section == 1:
            new_real = new_real * kern
            new_imag = new_imag * kern
        real_part = new_real.astype(jnp.bfloat16)
        imag_part = new_imag.astype(jnp.bfloat16)
    for section in range(2):
        rcos, rsin = turn(real_part, both)
        icos, isin = turn(imag_part, both)
        real_part = (rcos - isin).astype(jnp.bfloat16)
        imag_part = (icos + rsin).astype(jnp.bfloat16)
    rcos, rsin = turn(real_part, both)
    icos, isin = turn(imag_part, both)
    return rcos - isin


def exchange_term(chosen, target, both, kern):
    grid = both.shape[1]
    count = chosen.shape[0]
    pair = (chosen.astype(jnp.float32) * target.astype(jnp.float32)).astype(jnp.bfloat16)
    pair = pair.reshape(count, grid, grid * grid)
    field = potential(pair, both, kern).reshape(count, grid**3)
    return -jnp.sum(chosen.astype(jnp.float32) * field, axis=0, keepdims=True)


def shards(sources, targets):
    both = tables(GRID)
    kern = kernel_table(GRID)
    current = targets
    partial_value = None
    for step in range(HOPS):
        term = exchange_term(sources, current, both, kern)
        partial_value = term if partial_value is None else partial_value + term
        if step + 1 < HOPS:
            current = from_behind(current, "blk", 1)
            partial_value = from_behind(partial_value.astype(jnp.bfloat16), "blk", 1).astype(
                partial_value.dtype
            )
    summed = lax.psum_scatter(
        partial_value.astype(jnp.bfloat16), "wide", scatter_dimension=1, tiled=True
    ).astype(jnp.float32)
    return summed


def solution(mesh):
    in_specs = (P(("wide", "blk"), None), P("blk", None))
    out_specs = P("blk", "wide")
    return jax.shard_map(shards, mesh=mesh, in_specs=in_specs, out_specs=out_specs, check_vma=False)
```

profile of v0, /device:TPU:0, one launch (start us, length us, event | category | flops | bytes accessed | tf_op | source)
XLA Modules:
  0.0 185.9 jit_solution(6511493346900209224)
XLA Ops:
  6.5 3.1 %collective-permute-start.1 = (bf16[1,64000]{1,0:T(2,128)(2,1)}, bf16[1,64000]{1,0:T(2,128)(2,1)S(1)}, u32[]{:S(2)}, u32[]{:S(2)}) collective-permute-start(bf16[1,64000]{1,0:T(2,128)(2,1)} %param.3), channel_id=1, source_target_pairs={{3,0},{0,1},{1,2},{2,3},{7,4},{4,5},{5,6},{6,7},{11,8},{8,9},{9,10... | collective-permute-start | bytes 384008 | tf_op jit(solution)/shard_map/ppermute | solution.py:18
  9.8 0.3 add.349
  10.0 0.3 add.350
  10.3 7.7 %collective-permute-done.1 = bf16[1,64000]{1,0:T(2,128)(2,1)S(1)} collective-permute-done((bf16[1,64000]{1,0:T(2,128)(2,1)}, bf16[1,64000]{1,0:T(2,128)(2,1)S(1)}, u32[]{:S(2)}, u32[]{:S(2)}) %collective-permute-start.1) | collective-permute-done | bytes 128032 | tf_op jit(solution)/shard_map/ppermute | solution.py:18
  18.0 2.7 %convert_reduce_fusion.1 = (bf16[64000]{0:T(1024)(128)(2,1)S(1)}, bf16[64000]{0:T(1024)(128)(2,1)S(1)}) fusion(bf16[1,64000]{1,0:T(2,128)(2,1)} %param.3, bf16[1,64000]{1,0:T(2,128)(2,1)} %param.2, bf16[1,64000]{1,0:T(2,128)(2,1)S(1)} %collective-permute-done.1), kind=kLoop, calls=%fused_computation.44 | loop fusion | flops 448000 | bytes 640000 | tf_op jit(solution)/shard_map/convert_element_type | solution.py:74
  20.8 0.3 fusion.1
  21.5 0.3 fusion
  22.3 0.3 convert_element_type.324
  22.8 0.3 copy.26
  23.1 0.3 convert_element_type.326
  23.6 0.3 fusion.2
  23.9 0.3 fusion.3
  24.4 0.3 convert_element_type.330
  24.9 0.3 copy.27
  25.2 0.3 convert_element_type.328
  25.7 0.3 convolution_subtract_fusion.8
  26.0 0.3 convolution_add_fusion.6
  26.5 0.3 convert_element_type.347
  27.3 0.3 convert_element_type.349
  27.8 0.3 fusion.8
  28.1 0.3 fusion.9
  28.6 0.3 convert_element_type.353
  29.2 0.3 copy.38
  29.4 0.3 convert_element_type.351
  30.0 0.3 convolution_subtract_fusion.3
  30.2 0.3 convolution_add_fusion.2
  30.5 0.3 copy.40
  30.8 0.3 add.360
  31.0 0.3 copy.41
  31.3 0.3 sub.115
  31.6 0.3 copy.29
  31.9 0.3 add.343
  32.2 0.3 copy.30
  32.5 0.3 sub.108
  33.4 0.3 fusion.5
  33.7 0.3 fusion.4
  34.4 0.3 fusion.10
  34.7 0.4 fusion.11
  35.4 0.3 convert_element_type.359
  36.2 0.3 convert_element_type.357
  36.7 0.3 fusion.13
  37.0 0.3 fusion.12
  37.5 0.3 convert_element_type.361
  38.0 0.3 copy.45
  38.3 0.3 convert_element_type.363
  38.8 0.3 convert_element_type.335
  39.6 0.3 convert_element_type.337
  40.2 0.3 fusion.6
  40.4 0.3 fusion.7
  40.9 0.3 convert_element_type.341
  41.5 0.3 convert_element_type.339
  42.0 0.3 convolution_subtract_fusion.5
  42.3 0.3 copy.35
  42.6 0.7 sub.112
  43.3 0.4 negate_convert_fusion
  43.7 0.3 convolution_subtract_fusion
  44.0 0.3 copy.46
  44.3 0.7 sub.119
  45.0 7.8 %collective-permute-done = bf16[1,64000]{1,0:T(2,128)(2,1)S(1)} collective-permute-done((bf16[1,64000]{1,0:T(2,128)(2,1)S(1)}, bf16[1,64000]{1,0:T(2,128)(2,1)S(1)}, u32[]{:S(2)}, u32[]{:S(2)}) %collective-permute-start) | collective-permute-done | bytes 128032 | tf_op jit(solution)/shard_map/ppermute | solution.py:18
  52.9 0.5 add_convert_fusion
  53.4 10.5 %copy.47 = bf16[1,64000]{0,1:T(8,128)(2,1)} copy(bf16[1,64000]{1,0:T(2,128)(2,1)S(1)} %add_convert_fusion) | data formatting | bytes 256000
  63.9 112.5 %reduce-scatter.4.cloned.1.call-done = bf16[8000,1]{1,0:T(8,128)(2,1)} async-done(((bf16[64000,1]{1,0:T(8,128)(2,1)}), bf16[8000,1]{1,0:T(8,128)(2,1)}) %reduce-scatter.4.cloned.1.call-update) | async-done | bytes 16016
  176.4 2.0 %copy.48 = bf16[1,8000]{1,0:T(2,128)(2,1)S(1)} copy(bf16[1,8000]{0,1:T(8,128)(2,1)} %bitcast.43) | data formatting | bytes 32000
  178.4 0.6 convert_element_type.365
  (44 shorter events, 8.7 us)
Async XLA Ops:
  6.5 169.9 %reduce-scatter.4.cloned.1.call-start = ((), (), s32[]{:S(2)}) async-start(), calls=%async_computation.1 | async-start | bytes 18432000
  6.5 11.5 %collective-permute-start.1 = (bf16[1,64000]{1,0:T(2,128)(2,1)}, bf16[1,64000]{1,0:T(2,128)(2,1)S(1)}, u32[]{:S(2)}, u32[]{:S(2)}) collective-permute-start(bf16[1,64000]{1,0:T(2,128)(2,1)} %param.3), channel_id=1, source_target_pairs={{3,0},{0,1},{1,2},{2,3},{7,4},{4,5},{5,6},{6,7},{11,8},{8,9},{9,10... | collective-permute-start | bytes 384008 | tf_op jit(solution)/shard_map/ppermute | solution.py:18
  29.4 13.9 %copy-start = (bf16[1,64000]{1,0:T(2,128)(2,1)S(1)}, bf16[1,64000]{1,0:T(2,128)(2,1)}, u32[]{:S(2)}) copy-start(bf16[1,64000]{1,0:T(2,128)(2,1)} %param.2) | copy-start | bytes 384004
  43.7 9.2 %collective-permute-start = (bf16[1,64000]{1,0:T(2,128)(2,1)S(1)}, bf16[1,64000]{1,0:T(2,128)(2,1)S(1)}, u32[]{:S(2)}, u32[]{:S(2)}) collective-permute-start(bf16[1,64000]{1,0:T(2,128)(2,1)S(1)} %negate_convert_fusion), channel_id=1, source_target_pairs={{3,0},{0,1},{1,2},{2,3},{7,4},{4,5},{5,6},{6,7},{11,8},{8,9},{9,10... | collective-permute-start | bytes 384008 | tf_op jit(solution)/shard_map/ppermute | solution.py:18
Sparse Core Ops, SparseCore 0:
  64.0 112.3 reduce-scatter.3
where the time goes:
time: 186 us
  waiting for transfers between devices  128 us (69%)
  local copies, waits for them, and re-layouts  26 us (14%)
  between operations  14 us (8%)
  matrix products  10.3 us (6%)
  other arithmetic  4.43 us (2%)
  starting transfers between devices  3.11 us (2%)
    unnamed x2, waiting for transfers between devices  113 us
    ppermute x2, waiting for transfers between devices, from_behind(): return lax.ppermute(block, axis, route)  15.5 us
    unnamed x4, local copies, waits for them, and re-layouts  12.5 us
    dot_general x20, matrix products, turn(): jnp.einsum('mnr,kn->mrk', field, sin_table, preferred_element_type=jnp.fl...  5.35 us
    dot_general x20, matrix products, turn(): jnp.einsum('mnr,kn->mrk', field, cos_table, preferred_element_type=jnp.fl...  4.97 us
  transfers between devices with their start and end apart: 3, of which 3 were waited for; matrix products, arithmetic and copies ran while one was open for 1% of the time, Pallas kernels for 0%

commit v1 on v0

v1 whole, which is shorter than its diff:
```python
import functools
import math

import jax
import jax.numpy as jnp
import numpy as np
from jax import lax
from jax.experimental import pallas as pl
from jax.experimental.pallas import tpu as pltpu
from jax.sharding import PartitionSpec as P

MESH = pl.DeviceIdType.MESH
LANES = 128
SCREEN = 0.3
F32 = jnp.float32
BF16 = jnp.bfloat16


def basis(grid):
    half = grid // 2
    index = np.arange(grid)
    angle = 2.0 * math.pi / grid * ((index[:, None] * index[None, :]) % grid)
    cosines = np.cos(angle).astype(np.float32).astype(BF16).astype(np.float32)
    sines = np.sin(angle).astype(np.float32).astype(BF16).astype(np.float32)
    odd = np.arange(1, (grid + 1) // 2)
    q = np.concatenate([cosines[: half + 1], sines[odd]], axis=0)
    freq = np.concatenate([index[: half + 1], odd])
    weight = np.where(np.isin(freq, odd), 2.0, 1.0)
    return q, freq, weight


def plan(grid):
    q, freq, weight = basis(grid)
    group = max(d for d in range(1, grid + 1) if grid % d == 0 and d * grid <= 2 * LANES)
    per = grid // group
    wide = 2 * LANES
    a_mat = np.kron(q, np.eye(per))
    b_mat = np.kron(np.eye(group), q)
    c_mat = np.zeros((2, wide, group, LANES), np.float32)
    for h in range(2):
        lane = h * (LANES // 2)
        for j in range(group):
            c_mat[h, j * grid : (j + 1) * grid, j, lane : lane + grid] = q.T
    c_mat = c_mat.reshape(2 * wide, group * LANES)
    wave = 2.0 * math.pi / grid * freq
    sq = wave * wave
    total = sq[:, None, None] + sq[None, :, None] + sq[None, None, :]
    kern = 4.0 * math.pi / (total + SCREEN * SCREEN) / float(grid**3)
    kern = kern * weight[:, None, None] * weight[None, :, None] * weight[None, None, :]
    packed = np.zeros((grid // 2, grid, 2, LANES // 2), np.float32)
    for h in range(2):
        packed[:, :, h, :grid] = kern[h * (grid // 2) : (h + 1) * (grid // 2)]
    packed = packed.reshape(grid // 2 * grid, LANES)
    mats = [a_mat, a_mat.T, b_mat, b_mat.T, c_mat, c_mat.T]
    return group, [m.astype(BF16) for m in mats] + [packed.astype(np.float32)]


def dot(x, y):
    return jnp.dot(x, y, preferred_element_type=F32)


def exchange(pair, tables, y_ref, grid, group):
    a_ref, at_ref, b_ref, bt_ref, c_ref, ct_ref, k_ref = tables
    rows, wide = pair.shape
    hrows = rows // 2
    z = dot(a_ref[...], pair).astype(BF16)
    z = jnp.concatenate([z[:hrows], z[hrows:]], axis=1)
    y = dot(z, c_ref[...])
    for j in range(group):
        y_ref[pl.ds(j, hrows, stride=group), :] = y[:, j * LANES : (j + 1) * LANES]
    block = group * grid
    chunks = y_ref.shape[0] // block
    for i in range(0, chunks, 2):
        spans = [pl.ds(k * block, block) for k in (i, i + 1)]
        x = jnp.concatenate([y_ref[s, :].astype(BF16) for s in spans], axis=1)
        kern = jnp.concatenate([k_ref[s, :] for s in spans], axis=1)
        spec = (dot(b_ref[...], x) * kern).astype(BF16)
        back = dot(bt_ref[...], spec)
        for n, s in enumerate(spans):
            y_ref[s, :] = back[:, n * LANES : (n + 1) * LANES]
    x = jnp.concatenate(
        [y_ref[pl.ds(j, hrows, stride=group), :].astype(BF16) for j in range(group)], axis=1
    )
    z = dot(x, ct_ref[...]).astype(BF16)
    z = jnp.concatenate([z[:, :wide], z[:, wide:]], axis=0)
    return dot(at_ref[...], z)


def kernel(n_wide, n_blk, grid, group, src_ref, tgt_ref, *rest):
    tables = rest[:7]
    out_ref = rest[7]
    (y_ref, tgt_next, first_out, first_in, total, parts_out, parts_in,
     send_sem, recv_sem) = rest[8:]
    w = lax.axis_index("wide")
    b = lax.axis_index("blk")
    ahead = (w, lax.rem(b + 1, n_blk))
    behind = (w, lax.rem(b + n_blk - 1, n_blk))
    peers = [(lax.rem(w + d, n_wide), b) for d in range(1, n_wide)]
    barrier = pltpu.get_barrier_semaphore()
    greeted = [ahead, behind] + peers
    for device in greeted:
        pl.semaphore_signal(barrier, inc=1, device_id=device, device_id_type=MESH)
    pl.semaphore_wait(barrier, len(greeted))

    def send(src, dst, slot, device):
        copy = pltpu.make_async_remote_copy(
            src_ref=src, dst_ref=dst, send_sem=send_sem.at[slot], recv_sem=recv_sem.at[slot],
            device_id=device, device_id_type=MESH,
        )
        copy.start()
        return copy

    target_copy = send(tgt_ref, tgt_next, 0, ahead)
    source = src_ref[...].astype(F32)
    pair = (source * tgt_ref[...].astype(F32)).astype(BF16)
    term = source * exchange(pair, tables, y_ref, grid, group)
    first_out[...] = term.astype(BF16)
    first_copy = send(first_out, first_in, 1, ahead)
    target_copy.wait()
    source = src_ref[...].astype(F32)
    pair = (source * tgt_next[...].astype(F32)).astype(BF16)
    term = source * exchange(pair, tables, y_ref, grid, group)
    first_copy.wait()
    term = -(term + first_in[...].astype(F32))
    rows = term.shape[0] // n_wide
    for k in range(n_wide):
        piece = term[k * rows : (k + 1) * rows]
        total[k] = piece
        parts_out[k] = piece.astype(BF16)
    copies = [
        send(parts_out.at[peers[d][0]], parts_in.at[d], 2 + d, peers[d]) for d in range(n_wide - 1)
    ]
    summed = total[w]
    for d, copy in enumerate(copies):
        copy.wait()
        summed = summed + parts_in[d].astype(F32)
    out_ref[...] = summed


def shards(n_wide, n_blk, sources, targets):
    cells = sources.shape[1]
    grid = round(cells ** (1.0 / 3.0))
    group, tables = plan(grid)
    wide = 2 * LANES
    rows = cells // (group * grid)

    def laid(x):
        x = x.reshape(rows, group * grid)
        return jnp.pad(x, ((0, 0), (0, wide - group * grid)))

    part = rows // n_wide
    vmem = pl.BlockSpec(memory_space=pltpu.VMEM)
    result = pl.pallas_call(
        functools.partial(kernel, n_wide, n_blk, grid, group),
        out_shape=jax.ShapeDtypeStruct((part, wide), F32),
        in_specs=[vmem] * 9,
        out_specs=vmem,
        scratch_shapes=[
            pltpu.VMEM((rows // 2 * group, LANES), F32),
            pltpu.VMEM((rows, wide), BF16),
            pltpu.VMEM((rows, wide), BF16),
            pltpu.VMEM((rows, wide), BF16),
            pltpu.VMEM((n_wide, part, wide), F32),
            pltpu.VMEM((n_wide, part, wide), BF16),
            pltpu.VMEM((n_wide - 1, part, wide), BF16),
            pltpu.SemaphoreType.DMA((n_wide + 1,)),
            pltpu.SemaphoreType.DMA((n_wide + 1,)),
        ],
        compiler_params=pltpu.CompilerParams(collective_id=0, has_side_effects=True),
    )(laid(sources), laid(targets), *[jnp.asarray(t) for t in tables])
    return result[:, : group * grid].reshape(1, cells // n_wide)


def solution(mesh):
    body = functools.partial(shards, mesh.shape["wide"], mesh.shape["blk"])
    in_specs = (P(("wide", "blk"), None), P("blk", None))
    return jax.shard_map(
        body, mesh=mesh, in_specs=in_specs, out_specs=P("blk", "wide"), check_vma=False
    )
```

time: 186 us -> 27.4 us (0.15)
  waiting for transfers between devices: 128 us -> 0 us
  local copies, waits for them, and re-layouts: 26 us -> 3.81 us
  Pallas kernels: 0 us -> 20.9 us
  between operations: 14 us -> 0.04 us
  matrix products: 10.3 us -> 0 us
  starting transfers between devices: 3.11 us -> 0 us
  other arithmetic: 4.43 us -> 2.4 us
    unnamed x2 -> x0, waiting for transfers between devices: 113 us -> none
    pallas_call x0 -> x1, Pallas kernels: none -> 20.9 us  [shards(): pl.pallas_call(functools.partial(kernel, n_wide, n_blk, grid, group), out...]
    ppermute x2 -> x0, waiting for transfers between devices: 15.5 us -> none  [from_behind(): return lax.ppermute(block, axis, route)]
    unnamed x4 -> x2, local copies, waits for them, and re-layouts: 12.5 us -> 0.01 us
    dot_general x40 -> x0, matrix products: 10.3 us -> none  [the longest x20 5.35 us: turn(): jnp.einsum('mnr,kn->mrk', field, sin_table, preferred_element_type=jnp.fl...]
    convert_element_type x32 -> x0, local copies, waits for them, and re-layouts: 8.39 us -> none  [the longest x8 2.1 us: potential(): real_part = (rcos - isin).astype(jnp.bfloat16)]
    convert_element_type x5 -> x0, other arithmetic: 4.35 us -> none  [the longest x1 2.67 us: exchange_term(): (chosen.astype(jnp.float32) * target.astype(jnp.float32)).astype(jnp.bflo...]
    sub x8 -> x0, local copies, waits for them, and re-layouts: 3.13 us -> none  [the longest x4 2.03 us: potential(): return rcos - isin]
  transfers between devices with their start and end apart: 3 -> 0, of which waited for: 3 -> 0; matrix products, arithmetic and copies ran while one was open for 1% -> 0% of each run, Pallas kernels for 0% -> 0%
where the time goes in v1:
time: 27.4 us; the launch traced here: 27.2 us
  Pallas kernels  20.9 us (76%)
  local copies, waits for them, and re-layouts  3.81 us (14%)
  other arithmetic  2.4 us (9%)
    pallas_call x1, Pallas kernels, shards(): pl.pallas_call(functools.partial(kernel, n_wide, n_blk, grid, group), out...  20.9 us
    unnamed x2, other arithmetic  2.4 us
    reshape x1, local copies, waits for them, and re-layouts, shards(): return result[:, :group * grid].reshape(1, cells // n_wide)  1.52 us
    pad x2, local copies, waits for them, and re-layouts, laid(): return jnp.pad(x, ((0, 0), (0, wide - group * grid)))  1.36 us
    reshape x2, local copies, waits for them, and re-layouts, laid(): x = x.reshape(rows, group * grid)  0.93 us

profile of v1, /device:TPU:0, one launch (start us, length us, event | category | flops | bytes accessed | tf_op | source)
XLA Modules:
  0.0 27.2 jit_solution(16965941907646843471)
XLA Ops:
  0.0 1.7 %reduce = bf16[64000]{0:T(1024)(128)(2,1)S(1)} reduce(bf16[1,64000]{1,0:T(2,128)(2,1)} %param.9, bf16[]{:T(256)} %constant.30), dimensions={0}, to_apply=%param.9.reduce_sub_computation | reduce | bytes 256002 | tf_op args[0]
  1.7 0.0 copy-start
  1.7 0.5 %reshape.9 = bf16[320,200]{1,0:T(8,128)(2,1)S(1)} reshape(bf16[64000]{0:T(1024)(128)(2,1)S(1)} %reduce) | data formatting | bytes 256000 | tf_op jit(solution)/shard_map/reshape | solution.py:148
  2.1 0.7 %pad.7.src_ref = bf16[320,256]{1,0:T(8,128)(2,1)} pad(bf16[320,200]{1,0:T(8,128)(2,1)S(1)} %reshape.9, bf16[]{:T(256)} %constant.16.clone.1), padding=0_0x0_56 | pad | bytes 291842 | tf_op jit(solution)/shard_map/jit(_pad)/pad | solution.py:149
  2.8 0.0 copy-done
  2.8 0.7 %reduce.1 = bf16[64000]{0:T(1024)(128)(2,1)S(1)} reduce(bf16[1,64000]{1,0:T(2,128)(2,1)S(1)} %copy-done, bf16[]{:T(256)} %constant.30), dimensions={0}, to_apply=%param.10.reduce_sub_computation | reduce | bytes 256002 | tf_op args[1]
  3.6 0.5 %reshape.10 = bf16[320,200]{1,0:T(8,128)(2,1)S(1)} reshape(bf16[64000]{0:T(1024)(128)(2,1)S(1)} %reduce.1) | data formatting | bytes 256000 | tf_op jit(solution)/shard_map/reshape | solution.py:148
  4.0 0.7 %pad.8.tgt_ref = bf16[320,256]{1,0:T(8,128)(2,1)} pad(bf16[320,200]{1,0:T(8,128)(2,1)S(1)} %reshape.10, bf16[]{:T(256)} %constant.16.clone.1), padding=0_0x0_56 | pad | bytes 291842 | tf_op jit(solution)/shard_map/jit(_pad)/pad | solution.py:149
  4.7 20.9 %shard_map.91 = f32[40,256]{1,0:T(8,128)} custom-call(bf16[320,256]{1,0:T(8,128)(2,1)} %pad.7.src_ref, bf16[320,256]{1,0:T(8,128)(2,1)} %pad.8.tgt_ref, bf16[320,320]{1,0:T(8,128)(2,1)} %constant.17.clone.rest_0_, bf16[320,320]{1,0:T(8,128)(2,1)} %constant.18.clone.rest_1_, bf16[200,200]{1,0:T(8,128)(2,1)} %constant.19.clone.rest_2_, ...), custom_call_target="tpu_custom_call" | custom-call | tf_op jit(solution)/shard_map/pallas_call | solution.py:153
  25.6 1.5 %reshape.11 = f32[1,8000]{1,0:T(1,128)} reshape(f32[40,200]{1,0:T(8,128)} %bitcast.1) | data formatting | bytes 64000 | tf_op jit(solution)/shard_map/reshape | solution.py:171
Async XLA Ops:
  1.7 1.2 %copy-start = (bf16[1,64000]{1,0:T(2,128)(2,1)S(1)}, bf16[1,64000]{1,0:T(2,128)(2,1)}, u32[]{:S(2)}) copy-start(bf16[1,64000]{1,0:T(2,128)(2,1)} %param.10) | copy-start | bytes 384004

commit v2 on v1

--- a/solution.py
+++ b/solution.py
@@ -86,21 +86,51 @@
     return dot(at_ref[...], z)
 
 
+def relaid(raw_ref, flat_ref, z_ref, width):
+    flat_ref[...] = raw_ref[...].astype(F32).reshape(flat_ref.shape)
+    period = math.lcm(width, LANES)
+    tiles = period // LANES
+    lines = period // width
+    count = flat_ref.shape[0] // tiles
+    columns = [flat_ref[pl.ds(t, count, stride=tiles), :] for t in range(tiles)]
+    lane = lax.broadcasted_iota(jnp.int32, (count, LANES), 1)
+    for j in range(lines):
+        first, shift = divmod(width * j, LANES)
+        need = max(2, -(-(shift + width) // LANES))
+        x = jnp.concatenate(columns[first : first + need], axis=1)
+        if shift:
+            x = pltpu.roll(x, need * LANES - shift, 1)
+        for half in range(2):
+            piece = x[:, half * LANES : (half + 1) * LANES]
+            piece = jnp.where(lane + half * LANES < width, piece, 0.0)
+            z_ref[half, pl.ds(j, count, stride=lines), :] = piece
+    return jnp.concatenate([z_ref[0], z_ref[1]], axis=1)
+
+
 def kernel(n_wide, n_blk, grid, group, src_ref, tgt_ref, *rest):
-    tables = rest[:7]
+    table_hbm = rest[:7]
     out_ref = rest[7]
-    (y_ref, tgt_next, first_out, first_in, total, parts_out, parts_in,
-     send_sem, recv_sem) = rest[8:]
+    tables = rest[8:15]
+    (y_ref, flat_ref, z_ref, source_ref, tgt_out, tgt_in, total, parts_out, parts_in,
+     passed_out, passed_in, table_sem, send_sem, recv_sem) = rest[15:]
     w = lax.axis_index("wide")
     b = lax.axis_index("blk")
+    width = group * grid
+    loads = [
+        pltpu.make_async_copy(hbm, ref, table_sem.at[i])
+        for i, (hbm, ref) in enumerate(zip(table_hbm, tables))
+    ]
+    for load in loads:
+        load.start()
+    core = lax.rem(w, 2)
     ahead = (w, lax.rem(b + 1, n_blk))
     behind = (w, lax.rem(b + n_blk - 1, n_blk))
+    partner = (w + 1 - 2 * core, b)
     peers = [(lax.rem(w + d, n_wide), b) for d in range(1, n_wide)]
     barrier = pltpu.get_barrier_semaphore()
     greeted = [ahead, behind] + peers
     for device in greeted:
         pl.semaphore_signal(barrier, inc=1, device_id=device, device_id_type=MESH)
-    pl.semaphore_wait(barrier, len(greeted))
 
     def send(src, dst, slot, device):
         copy = pltpu.make_async_remote_copy(
@@ -110,31 +140,55 @@
         copy.start()
         return copy
 
-    target_copy = send(tgt_ref, tgt_next, 0, ahead)
-    source = src_ref[...].astype(F32)
-    pair = (source * tgt_ref[...].astype(F32)).astype(BF16)
-    term = source * exchange(pair, tables, y_ref, grid, group)
-    first_out[...] = term.astype(BF16)
-    first_copy = send(first_out, first_in, 1, ahead)
-    target_copy.wait()
-    source = src_ref[...].astype(F32)
-    pair = (source * tgt_next[...].astype(F32)).astype(BF16)
-    term = source * exchange(pair, tables, y_ref, grid, group)
-    first_copy.wait()
-    term = -(term + first_in[...].astype(F32))
-    rows = term.shape[0] // n_wide
-    for k in range(n_wide):
-        piece = term[k * rows : (k + 1) * rows]
-        total[k] = piece
-        parts_out[k] = piece.astype(BF16)
-    copies = [
-        send(parts_out.at[peers[d][0]], parts_in.at[d], 2 + d, peers[d]) for d in range(n_wide - 1)
+    target = relaid(tgt_ref, flat_ref, z_ref, width)
+    tgt_out[...] = target.reshape(tgt_out.shape).astype(BF16)
+    quarter = tgt_out.shape[0] // 2
+    pl.semaphore_wait(barrier, len(greeted))
+    hops = [
+        send(tgt_out.at[core * quarter + k], tgt_in.at[core * quarter + k], k, ahead)
+        for k in range(quarter)
     ]
-    summed = total[w]
-    for d, copy in enumerate(copies):
-        copy.wait()
-        summed = summed + parts_in[d].astype(F32)
-    out_ref[...] = summed
+    source = relaid(src_ref, flat_ref, z_ref, width)
+    source_ref[...] = source
+    for load in loads:
+        load.wait()
+    rows = source.shape[0] // n_wide
+
+    def scatter(target, turn):
+        pair = (source_ref[...] * target).astype(BF16)
+        term = source_ref[...] * exchange(pair, tables, y_ref, grid, group)
+        for k in range(n_wide):
+            piece = term[k * rows : (k + 1) * rows]
+            total[turn, k] = piece
+            parts_out[turn, k] = piece.astype(BF16)
+        slot = 2 * quarter + 1 + turn * (n_wide - 1)
+        return [
+            send(parts_out.at[turn, peers[d][0]], parts_in.at[turn, d], slot + d, peers[d])
+            for d in range(n_wide - 1)
+        ]
+
+    def gathered(copies, turn):
+        summed = total[turn, w]
+        for d, copy in enumerate(copies):
+            copy.wait()
+            summed = summed + parts_in[turn, d].astype(F32)
+        return summed
+
+    first = scatter(target, 0)
+    relays = []
+    for k, hop in enumerate(hops):
+        hop.wait()
+        here = tgt_in.at[core * quarter + k]
+        relays.append(send(here, here, quarter + k, partner))
+    passed_out[...] = gathered(first, 0).astype(BF16)
+    passed = send(passed_out, passed_in, 2 * quarter, ahead)
+    for relay in relays:
+        relay.wait()
+    second = scatter(tgt_in[...].astype(F32).reshape(source.shape), 1)
+    passed.wait()
+    summed = -(gathered(second, 1) + passed_in[...].astype(F32))
+    for k in range(rows):
+        out_ref[0:1, k * width : (k + 1) * width] = summed[k : k + 1, :width]
 
 
 def shards(n_wide, n_blk, sources, targets):
@@ -143,32 +197,35 @@
     group, tables = plan(grid)
     wide = 2 * LANES
     rows = cells // (group * grid)
-
-    def laid(x):
-        x = x.reshape(rows, group * grid)
-        return jnp.pad(x, ((0, 0), (0, wide - group * grid)))
-
     part = rows // n_wide
+    line = 8 * (rows // 64)
     vmem = pl.BlockSpec(memory_space=pltpu.VMEM)
-    result = pl.pallas_call(
+    hbm = pl.BlockSpec(memory_space=pl.ANY)
+    sems = 2 * (rows // line // 2) + 1 + 2 * (n_wide - 1)
+    return pl.pallas_call(
         functools.partial(kernel, n_wide, n_blk, grid, group),
-        out_shape=jax.ShapeDtypeStruct((part, wide), F32),
-        in_specs=[vmem] * 9,
+        out_shape=jax.ShapeDtypeStruct((1, cells // n_wide), F32),
+        in_specs=[vmem] * 2 + [hbm] * 7,
         out_specs=vmem,
-        scratch_shapes=[
+        scratch_shapes=[pltpu.VMEM(t.shape, t.dtype) for t in tables]
+        + [
             pltpu.VMEM((rows // 2 * group, LANES), F32),
-            pltpu.VMEM((rows, wide), BF16),
-            pltpu.VMEM((rows, wide), BF16),
-            pltpu.VMEM((rows, wide), BF16),
-            pltpu.VMEM((n_wide, part, wide), F32),
-            pltpu.VMEM((n_wide, part, wide), BF16),
-            pltpu.VMEM((n_wide - 1, part, wide), BF16),
-            pltpu.SemaphoreType.DMA((n_wide + 1,)),
-            pltpu.SemaphoreType.DMA((n_wide + 1,)),
+            pltpu.VMEM((cells // LANES, LANES), F32),
+            pltpu.VMEM((2, rows, LANES), F32),
+            pltpu.VMEM((rows, wide), F32),
+            pltpu.VMEM((rows // line, line, wide), BF16),
+            pltpu.VMEM((rows // line, line, wide), BF16),
+            pltpu.VMEM((2, n_wide, part, wide), F32),
+            pltpu.VMEM((2, n_wide, part, wide), BF16),
+            pltpu.VMEM((2, n_wide - 1, part, wide), BF16),
+            pltpu.VMEM((part, wide), BF16),
+            pltpu.VMEM((part, wide), BF16),
+            pltpu.SemaphoreType.DMA((len(tables),)),
+            pltpu.SemaphoreType.DMA((sems,)),
+            pltpu.SemaphoreType.DMA((sems,)),
         ],
         compiler_params=pltpu.CompilerParams(collective_id=0, has_side_effects=True),
-    )(laid(sources), laid(targets), *[jnp.asarray(t) for t in tables])
-    return result[:, : group * grid].reshape(1, cells // n_wide)
+    )(sources, targets, *[jnp.asarray(t) for t in tables])
 
 
 def solution(mesh):

time: 27.4 us -> 19.9 us (0.73)
  Pallas kernels: 20.9 us -> 18.3 us
  local copies, waits for them, and re-layouts: 3.81 us -> 1.37 us
  other arithmetic: 2.4 us -> 0 us
    pallas_call x1, Pallas kernels: 20.9 us -> 18.3 us  [shards(): pl.pallas_call(functools.partial(kernel, n_wide, n_blk, grid, group), out...]
    reshape x3 -> x0, local copies, waits for them, and re-layouts: 2.44 us -> none  [the longest x1 1.52 us: shards(): return result[:, :group * grid].reshape(1, cells // n_wide)]
    unnamed x2 -> x0, other arithmetic: 2.4 us -> none
    unnamed x2 -> x1, local copies, waits for them, and re-layouts: 0.01 us -> 1.37 us
    pad x2 -> x0, local copies, waits for them, and re-layouts: 1.36 us -> none  [laid(): return jnp.pad(x, ((0, 0), (0, wide - group * grid)))]
where the time goes in v2:
time: 19.9 us; the launch traced here: 19.7 us
  Pallas kernels  18.3 us (92%)
  local copies, waits for them, and re-layouts  1.37 us (7%)
    pallas_call x1, Pallas kernels, shards(): pl.pallas_call(functools.partial(kernel, n_wide, n_blk, grid, group), out...  18.3 us
    unnamed x1, local copies, waits for them, and re-layouts  1.37 us

profile of v2, /device:TPU:0, one launch (start us, length us, event | category | flops | bytes accessed | tf_op | source)
XLA Modules:
  0.0 19.7 jit_solution(16158437996744073377)
XLA Ops:
  0.0 18.3 %shard_map.91 = f32[1,8000]{1,0:T(1,128)} custom-call(bf16[1,64000]{1,0:T(2,128)(2,1)} %src_ref.1, bf16[1,64000]{1,0:T(2,128)(2,1)} %tgt_ref.1, bf16[320,320]{1,0:T(8,128)(2,1)} %constant.14.clone.rest_0_, bf16[320,320]{1,0:T(8,128)(2,1)} %constant.15.clone.rest_1_, bf16[200,200]{1,0:T(8,128)(2,1)} %constant.16.clone.rest_2_, ...), custom_call_target="tpu_custom_call" | custom-call | tf_op jit(solution)/shard_map/pallas_call | solution.py:205
  18.3 1.4 %copy.11 = f32[1,8000]{1,0:T(1,128)} copy(f32[1,8000]{1,0:T(1,128)} %shard_map.91) | data formatting | bytes 64000

commit v3 on v2

--- a/solution.py
+++ b/solution.py
@@ -107,28 +107,47 @@
     return jnp.concatenate([z_ref[0], z_ref[1]], axis=1)
 
 
-def kernel(n_wide, n_blk, grid, group, src_ref, tgt_ref, *rest):
+def partners(w, n_wide):
+    if n_wide & (n_wide - 1):
+        return [(lax.rem(w + d, n_wide), d - 1) for d in range(1, n_wide)]
+    bits = [1 << k for k in range(n_wide.bit_length() - 1)]
+    found = []
+    for d in range(1, n_wide):
+        flips = [bit for bit in bits if d & bit]
+        other = w
+        for bit in flips:
+            other = other + bit - 2 * bit * lax.rem(w // bit, 2)
+        found.append((len([bit for bit in flips if bit > 1]), d, other))
+    found.sort(key=lambda item: (-item[0], item[1]))
+    return [(other, d - 1) for _, d, other in found]
+
+
+def kernel(n_wide, n_blk, grid, group, src_hbm, tgt_hbm, *rest):
     table_hbm = rest[:7]
     out_ref = rest[7]
     tables = rest[8:15]
-    (y_ref, flat_ref, z_ref, source_ref, tgt_out, tgt_in, total, parts_out, parts_in,
-     passed_out, passed_in, table_sem, send_sem, recv_sem) = rest[15:]
+    (src_ref, tgt_ref, y_ref, flat_ref, z_ref, source_ref, tgt_out, tgt_in, total, parts_out, parts_in,
+     passed_out, passed_in, raw_sem, table_sem, send_sem, recv_sem) = rest[15:]
     w = lax.axis_index("wide")
     b = lax.axis_index("blk")
     width = group * grid
+    raw = [
+        pltpu.make_async_copy(hbm, ref, raw_sem.at[i])
+        for i, (hbm, ref) in enumerate(((tgt_hbm, tgt_ref), (src_hbm, src_ref)))
+    ]
+    for load in raw:
+        load.start()
     loads = [
         pltpu.make_async_copy(hbm, ref, table_sem.at[i])
         for i, (hbm, ref) in enumerate(zip(table_hbm, tables))
     ]
-    for load in loads:
-        load.start()
     core = lax.rem(w, 2)
     ahead = (w, lax.rem(b + 1, n_blk))
     behind = (w, lax.rem(b + n_blk - 1, n_blk))
     partner = (w + 1 - 2 * core, b)
-    peers = [(lax.rem(w + d, n_wide), b) for d in range(1, n_wide)]
+    peers = partners(w, n_wide)
     barrier = pltpu.get_barrier_semaphore()
-    greeted = [ahead, behind] + peers
+    greeted = [ahead, behind] + [(other, b) for other, _ in peers]
     for device in greeted:
         pl.semaphore_signal(barrier, inc=1, device_id=device, device_id_type=MESH)
 
@@ -140,6 +159,9 @@
         copy.start()
         return copy
 
+    for load in loads:
+        load.start()
+    raw[0].wait()
     target = relaid(tgt_ref, flat_ref, z_ref, width)
     tgt_out[...] = target.reshape(tgt_out.shape).astype(BF16)
     quarter = tgt_out.shape[0] // 2
@@ -148,6 +170,7 @@
         send(tgt_out.at[core * quarter + k], tgt_in.at[core * quarter + k], k, ahead)
         for k in range(quarter)
     ]
+    raw[1].wait()
     source = relaid(src_ref, flat_ref, z_ref, width)
     source_ref[...] = source
     for load in loads:
@@ -163,13 +186,13 @@
             parts_out[turn, k] = piece.astype(BF16)
         slot = 2 * quarter + 1 + turn * (n_wide - 1)
         return [
-            send(parts_out.at[turn, peers[d][0]], parts_in.at[turn, d], slot + d, peers[d])
-            for d in range(n_wide - 1)
+            send(parts_out.at[turn, other], parts_in.at[turn, d], slot + d, (other, b))
+            for other, d in peers
         ]
 
     def gathered(copies, turn):
         summed = total[turn, w]
-        for d, copy in enumerate(copies):
+        for (_, d), copy in reversed(list(zip(peers, copies))):
             copy.wait()
             summed = summed + parts_in[turn, d].astype(F32)
         return summed
@@ -180,13 +203,14 @@
         hop.wait()
         here = tgt_in.at[core * quarter + k]
         relays.append(send(here, here, quarter + k, partner))
-    passed_out[...] = gathered(first, 0).astype(BF16)
-    passed = send(passed_out, passed_in, 2 * quarter, ahead)
     for relay in relays:
         relay.wait()
     second = scatter(tgt_in[...].astype(F32).reshape(source.shape), 1)
+    passed_out[...] = gathered(first, 0).astype(BF16)
+    passed = send(passed_out, passed_in, 2 * quarter, ahead)
+    summed = gathered(second, 1)
     passed.wait()
-    summed = -(gathered(second, 1) + passed_in[...].astype(F32))
+    summed = -(summed + passed_in[...].astype(F32))
     for k in range(rows):
         out_ref[0:1, k * width : (k + 1) * width] = summed[k : k + 1, :width]
 
@@ -205,10 +229,12 @@
     return pl.pallas_call(
         functools.partial(kernel, n_wide, n_blk, grid, group),
         out_shape=jax.ShapeDtypeStruct((1, cells // n_wide), F32),
-        in_specs=[vmem] * 2 + [hbm] * 7,
+        in_specs=[hbm] * 9,
         out_specs=vmem,
         scratch_shapes=[pltpu.VMEM(t.shape, t.dtype) for t in tables]
         + [
+            pltpu.VMEM((1, cells), BF16),
+            pltpu.VMEM((1, cells), BF16),
             pltpu.VMEM((rows // 2 * group, LANES), F32),
             pltpu.VMEM((cells // LANES, LANES), F32),
             pltpu.VMEM((2, rows, LANES), F32),
@@ -220,6 +246,7 @@
             pltpu.VMEM((2, n_wide - 1, part, wide), BF16),
             pltpu.VMEM((part, wide), BF16),
             pltpu.VMEM((part, wide), BF16),
+            pltpu.SemaphoreType.DMA((2,)),
             pltpu.SemaphoreType.DMA((len(tables),)),
             pltpu.SemaphoreType.DMA((sems,)),
             pltpu.SemaphoreType.DMA((sems,)),

time: 19.9 us -> 18.6 us (0.935)
  Pallas kernels: 18.3 us -> 17.1 us
    pallas_call x1, Pallas kernels: 18.3 us -> 17.1 us  [shards(): pl.pallas_call(functools.partial(kernel, n_wide, n_blk, grid, group), out...]
where the time goes in v3:
time: 18.6 us; the launch traced here: 18.4 us
  Pallas kernels  17.1 us (92%)
  local copies, waits for them, and re-layouts  1.37 us (7%)
    pallas_call x1, Pallas kernels, shards(): pl.pallas_call(functools.partial(kernel, n_wide, n_blk, grid, group), out...  17.1 us
    unnamed x1, local copies, waits for them, and re-layouts  1.37 us

profile of v3, /device:TPU:0, one launch (start us, length us, event | category | flops | bytes accessed | tf_op | source)
XLA Modules:
  0.0 18.4 jit_solution(2287831119686821608)
XLA Ops:
  0.0 17.1 %shard_map.91 = f32[1,8000]{1,0:T(1,128)} custom-call(bf16[1,64000]{1,0:T(2,128)(2,1)} %src_hbm.1, bf16[1,64000]{1,0:T(2,128)(2,1)} %tgt_hbm.1, bf16[320,320]{1,0:T(8,128)(2,1)} %constant.14.clone.rest_0_, bf16[320,320]{1,0:T(8,128)(2,1)} %constant.15.clone.rest_1_, bf16[200,200]{1,0:T(8,128)(2,1)} %constant.16.clone.rest_2_, ...), custom_call_target="tpu_custom_call" | custom-call | tf_op jit(solution)/shard_map/pallas_call | solution.py:229
  17.1 1.4 %copy.11 = f32[1,8000]{1,0:T(1,128)} copy(f32[1,8000]{1,0:T(1,128)} %shard_map.91) | data formatting | bytes 64000

commit v4 on v3

--- a/solution.py
+++ b/solution.py
@@ -87,7 +87,10 @@
 
 
 def relaid(raw_ref, flat_ref, z_ref, width):
-    flat_ref[...] = raw_ref[...].astype(F32).reshape(flat_ref.shape)
+    for first in range(0, flat_ref.shape[0], 8):
+        some = min(8, flat_ref.shape[0] - first)
+        part = raw_ref[:, first * LANES : (first + some) * LANES]
+        flat_ref[first : first + some, :] = part.astype(F32).reshape(some, LANES)
     period = math.lcm(width, LANES)
     tiles = period // LANES
     lines = period // width
@@ -210,7 +213,7 @@
     passed = send(passed_out, passed_in, 2 * quarter, ahead)
     summed = gathered(second, 1)
     passed.wait()
-    summed = -(summed + passed_in[...].astype(F32))
+    summed = summed + passed_in[...].astype(F32)
     for k in range(rows):
         out_ref[0:1, k * width : (k + 1) * width] = summed[k : k + 1, :width]
 
@@ -224,11 +227,11 @@
     part = rows // n_wide
     line = 8 * (rows // 64)
     vmem = pl.BlockSpec(memory_space=pltpu.VMEM)
-    hbm = pl.BlockSpec(memory_space=pl.ANY)
+    hbm = pl.BlockSpec(memory_space=pltpu.HBM)
     sems = 2 * (rows // line // 2) + 1 + 2 * (n_wide - 1)
-    return pl.pallas_call(
+    result = pl.pallas_call(
         functools.partial(kernel, n_wide, n_blk, grid, group),
-        out_shape=jax.ShapeDtypeStruct((1, cells // n_wide), F32),
+        out_shape=pltpu.VMEM((1, cells // n_wide), F32),
         in_specs=[hbm] * 9,
         out_specs=vmem,
         scratch_shapes=[pltpu.VMEM(t.shape, t.dtype) for t in tables]
@@ -251,8 +254,9 @@
             pltpu.SemaphoreType.DMA((sems,)),
             pltpu.SemaphoreType.DMA((sems,)),
         ],
-        compiler_params=pltpu.CompilerParams(collective_id=0, has_side_effects=True),
+        compiler_params=pltpu.CompilerParams(collective_id=0, has_side_effects=True, vmem_limit_bytes=56 << 20),
     )(sources, targets, *[jnp.asarray(t) for t in tables])
+    return -result
 
 
 def solution(mesh):

time: 18.6 us -> 17.2 us (0.925)
  local copies, waits for them, and re-layouts: 1.37 us -> 0 us
  other arithmetic: 0 us -> 0.64 us
  Pallas kernels: 17.1 us -> 16.5 us
    unnamed x1 -> x0, local copies, waits for them, and re-layouts: 1.37 us -> none
    neg x0 -> x1, other arithmetic: none -> 0.64 us  [shards(): return -result]
    pallas_call x1, Pallas kernels: 17.1 us -> 16.5 us  [shards(): pl.pallas_call(functools.partial(kernel, n_wide, n_blk, grid, group), out...]
where the time goes in v4:
time: 17.2 us; the launch traced here: 17.1 us
  Pallas kernels  16.5 us (96%)
  other arithmetic  0.64 us (4%)
    pallas_call x1, Pallas kernels, shards(): pl.pallas_call(functools.partial(kernel, n_wide, n_blk, grid, group), out...  16.5 us
    neg x1, other arithmetic, shards(): return -result  0.64 us

profile of v4, /device:TPU:0, one launch (start us, length us, event | category | flops | bytes accessed | tf_op | source)
XLA Modules:
  0.0 17.1 jit_solution(14220630199523940584)
XLA Ops:
  0.0 16.5 %shard_map.91 = f32[1,8000]{1,0:T(1,128)S(1)} custom-call(bf16[1,64000]{1,0:T(2,128)(2,1)} %src_hbm.1, bf16[1,64000]{1,0:T(2,128)(2,1)} %tgt_hbm.1, bf16[320,320]{1,0:T(8,128)(2,1)} %constant.14.clone.rest_0_, bf16[320,320]{1,0:T(8,128)(2,1)} %constant.15.clone.rest_1_, bf16[200,200]{1,0:T(8,128)(2,1)} %constant.16.clone.rest_2_, ...), custom_call_target="tpu_custom_call" | custom-call | tf_op jit(solution)/shard_map/pallas_call | solution.py:232
  16.5 0.6 %neg.3 = f32[1,8000]{1,0:T(1,128)} negate(f32[1,8000]{1,0:T(1,128)S(1)} %shard_map.91) | non-fusion elementwise | flops 8000 | bytes 64000 | tf_op jit(solution)/shard_map/neg | solution.py:259

commit v5 on v4

--- a/solution.py
+++ b/solution.py
@@ -86,15 +86,21 @@
     return dot(at_ref[...], z)
 
 
-def relaid(raw_ref, flat_ref, z_ref, width):
-    for first in range(0, flat_ref.shape[0], 8):
-        some = min(8, flat_ref.shape[0] - first)
+def flattened(raw_ref, flat_ref):
+    lines = raw_ref.shape[1] // LANES
+    for first in range(0, lines, 8):
+        some = min(8, lines - first)
         part = raw_ref[:, first * LANES : (first + some) * LANES]
         flat_ref[first : first + some, :] = part.astype(F32).reshape(some, LANES)
+    if flat_ref.shape[0] > lines:
+        flat_ref[lines:, :] = jnp.zeros((flat_ref.shape[0] - lines, LANES), F32)
+
+
+def relaid(flat_ref, z_ref, width):
     period = math.lcm(width, LANES)
     tiles = period // LANES
     lines = period // width
-    count = flat_ref.shape[0] // tiles
+    count = z_ref.shape[1] // lines
     columns = [flat_ref[pl.ds(t, count, stride=tiles), :] for t in range(tiles)]
     lane = lax.broadcasted_iota(jnp.int32, (count, LANES), 1)
     for j in range(lines):
@@ -148,9 +154,10 @@
     ahead = (w, lax.rem(b + 1, n_blk))
     behind = (w, lax.rem(b + n_blk - 1, n_blk))
     partner = (w + 1 - 2 * core, b)
+    across = (partner[0], ahead[1])
     peers = partners(w, n_wide)
     barrier = pltpu.get_barrier_semaphore()
-    greeted = [ahead, behind] + [(other, b) for other, _ in peers]
+    greeted = [ahead, behind, across, (partner[0], behind[1])] + [(other, b) for other, _ in peers]
     for device in greeted:
         pl.semaphore_signal(barrier, inc=1, device_id=device, device_id_type=MESH)
 
@@ -165,16 +172,18 @@
     for load in loads:
         load.start()
     raw[0].wait()
-    target = relaid(tgt_ref, flat_ref, z_ref, width)
-    tgt_out[...] = target.reshape(tgt_out.shape).astype(BF16)
+    flattened(tgt_ref, flat_ref)
+    tgt_out[...] = flat_ref[...].astype(BF16).reshape(tgt_out.shape)
     quarter = tgt_out.shape[0] // 2
+    mine = core * quarter
+    last = mine + quarter - 1
     pl.semaphore_wait(barrier, len(greeted))
-    hops = [
-        send(tgt_out.at[core * quarter + k], tgt_in.at[core * quarter + k], k, ahead)
-        for k in range(quarter)
-    ]
+    hops = [send(tgt_out.at[mine + k], tgt_in.at[mine + k], k, ahead) for k in range(quarter)]
+    direct = send(tgt_out.at[last], tgt_in.at[last], 2 * quarter - 1, across)
+    target = relaid(flat_ref, z_ref, width)
     raw[1].wait()
-    source = relaid(src_ref, flat_ref, z_ref, width)
+    flattened(src_ref, flat_ref)
+    source = relaid(flat_ref, z_ref, width)
     source_ref[...] = source
     for load in loads:
         load.wait()
@@ -204,11 +213,14 @@
     relays = []
     for k, hop in enumerate(hops):
         hop.wait()
-        here = tgt_in.at[core * quarter + k]
-        relays.append(send(here, here, quarter + k, partner))
+        if k < quarter - 1:
+            here = tgt_in.at[mine + k]
+            relays.append(send(here, here, quarter + k, partner))
     for relay in relays:
         relay.wait()
-    second = scatter(tgt_in[...].astype(F32).reshape(source.shape), 1)
+    direct.wait()
+    flat_ref[...] = tgt_in[...].astype(F32).reshape(flat_ref.shape)
+    second = scatter(relaid(flat_ref, z_ref, width), 1)
     passed_out[...] = gathered(first, 0).astype(BF16)
     passed = send(passed_out, passed_in, 2 * quarter, ahead)
     summed = gathered(second, 1)
@@ -225,10 +237,10 @@
     wide = 2 * LANES
     rows = cells // (group * grid)
     part = rows // n_wide
-    line = 8 * (rows // 64)
+    line = 8 * -(-cells // (64 * LANES))
     vmem = pl.BlockSpec(memory_space=pltpu.VMEM)
     hbm = pl.BlockSpec(memory_space=pltpu.HBM)
-    sems = 2 * (rows // line // 2) + 1 + 2 * (n_wide - 1)
+    sems = 8 + 1 + 2 * (n_wide - 1)
     result = pl.pallas_call(
         functools.partial(kernel, n_wide, n_blk, grid, group),
         out_shape=pltpu.VMEM((1, cells // n_wide), F32),
@@ -239,11 +251,11 @@
             pltpu.VMEM((1, cells), BF16),
             pltpu.VMEM((1, cells), BF16),
             pltpu.VMEM((rows // 2 * group, LANES), F32),
-            pltpu.VMEM((cells // LANES, LANES), F32),
+            pltpu.VMEM((8 * line, LANES), F32),
             pltpu.VMEM((2, rows, LANES), F32),
             pltpu.VMEM((rows, wide), F32),
-            pltpu.VMEM((rows // line, line, wide), BF16),
-            pltpu.VMEM((rows // line, line, wide), BF16),
+            pltpu.VMEM((8, line, LANES), BF16),
+            pltpu.VMEM((8, line, LANES), BF16),
             pltpu.VMEM((2, n_wide, part, wide), F32),
             pltpu.VMEM((2, n_wide, part, wide), BF16),
             pltpu.VMEM((2, n_wide - 1, part, wide), BF16),

time: 17.2 us -> 17.1 us (level)
  Pallas kernels: 16.5 us -> 16.3 us
where the time goes in v5:
time: 17.1 us; the launch traced here: 16.9 us
  Pallas kernels  16.3 us (95%)
  other arithmetic  0.64 us (4%)
    pallas_call x1, Pallas kernels, shards(): pl.pallas_call(functools.partial(kernel, n_wide, n_blk, grid, group), out...  16.3 us
    neg x1, other arithmetic, shards(): return -result  0.64 us

profile of v5, /device:TPU:0, one launch (start us, length us, event | category | flops | bytes accessed | tf_op | source)
XLA Modules:
  0.0 16.9 jit_solution(7555093402672204120)
XLA Ops:
  0.0 16.3 %shard_map.91 = f32[1,8000]{1,0:T(1,128)S(1)} custom-call(bf16[1,64000]{1,0:T(2,128)(2,1)} %src_hbm.1, bf16[1,64000]{1,0:T(2,128)(2,1)} %tgt_hbm.1, bf16[320,320]{1,0:T(8,128)(2,1)} %constant.14.clone.rest_0_, bf16[320,320]{1,0:T(8,128)(2,1)} %constant.15.clone.rest_1_, bf16[200,200]{1,0:T(8,128)(2,1)} %constant.16.clone.rest_2_, ...), custom_call_target="tpu_custom_call" | custom-call | tf_op jit(solution)/shard_map/pallas_call | solution.py:244
  16.3 0.6 %neg.3 = f32[1,8000]{1,0:T(1,128)} negate(f32[1,8000]{1,0:T(1,128)S(1)} %shard_map.91) | non-fusion elementwise | flops 8000 | bytes 64000 | tf_op jit(solution)/shard_map/neg | solution.py:271

commit v6 on v5

--- a/solution.py
+++ b/solution.py
@@ -157,7 +157,7 @@
     across = (partner[0], ahead[1])
     peers = partners(w, n_wide)
     barrier = pltpu.get_barrier_semaphore()
-    greeted = [ahead, behind, across, (partner[0], behind[1])] + [(other, b) for other, _ in peers]
+    greeted = [behind, (partner[0], behind[1])] + [(other, b) for other, _ in peers]
     for device in greeted:
         pl.semaphore_signal(barrier, inc=1, device_id=device, device_id_type=MESH)
 

time: 17.1 us -> 17.1 us (level)
  no operation moved by 1% of the time
where the time goes in v6:
time: 17.1 us; the launch traced here: 16.9 us
  Pallas kernels  16.3 us (95%)
  other arithmetic  0.64 us (4%)
    pallas_call x1, Pallas kernels, shards(): pl.pallas_call(functools.partial(kernel, n_wide, n_blk, grid, group), out...  16.3 us
    neg x1, other arithmetic, shards(): return -result  0.64 us

profile of v6, /device:TPU:0, one launch (start us, length us, event | category | flops | bytes accessed | tf_op | source)
XLA Modules:
  0.0 16.9 jit_solution(11989709602125999464)
XLA Ops:
  0.0 16.3 %shard_map.91 = f32[1,8000]{1,0:T(1,128)S(1)} custom-call(bf16[1,64000]{1,0:T(2,128)(2,1)} %src_hbm.1, bf16[1,64000]{1,0:T(2,128)(2,1)} %tgt_hbm.1, bf16[320,320]{1,0:T(8,128)(2,1)} %constant.14.clone.rest_0_, bf16[320,320]{1,0:T(8,128)(2,1)} %constant.15.clone.rest_1_, bf16[200,200]{1,0:T(8,128)(2,1)} %constant.16.clone.rest_2_, ...), custom_call_target="tpu_custom_call" | custom-call | tf_op jit(solution)/shard_map/pallas_call | solution.py:244
  16.3 0.6 %neg.3 = f32[1,8000]{1,0:T(1,128)} negate(f32[1,8000]{1,0:T(1,128)S(1)} %shard_map.91) | non-fusion elementwise | flops 8000 | bytes 64000 | tf_op jit(solution)/shard_map/neg | solution.py:271

commit v7 on v6

--- a/solution.py
+++ b/solution.py
@@ -135,7 +135,7 @@
     table_hbm = rest[:7]
     out_ref = rest[7]
     tables = rest[8:15]
-    (src_ref, tgt_ref, y_ref, flat_ref, z_ref, source_ref, tgt_out, tgt_in, total, parts_out, parts_in,
+    (src_ref, tgt_ref, y_ref, flat_ref, z_ref, source_ref, tgt_out, tgt_in, parts_out, parts_in,
      passed_out, passed_in, raw_sem, table_sem, send_sem, recv_sem) = rest[15:]
     w = lax.axis_index("wide")
     b = lax.axis_index("blk")
@@ -193,9 +193,7 @@
         pair = (source_ref[...] * target).astype(BF16)
         term = source_ref[...] * exchange(pair, tables, y_ref, grid, group)
         for k in range(n_wide):
-            piece = term[k * rows : (k + 1) * rows]
-            total[turn, k] = piece
-            parts_out[turn, k] = piece.astype(BF16)
+            parts_out[turn, k] = term[k * rows : (k + 1) * rows].astype(BF16)
         slot = 2 * quarter + 1 + turn * (n_wide - 1)
         return [
             send(parts_out.at[turn, other], parts_in.at[turn, d], slot + d, (other, b))
@@ -203,7 +201,7 @@
         ]
 
     def gathered(copies, turn):
-        summed = total[turn, w]
+        summed = parts_out[turn, w].astype(F32)
         for (_, d), copy in reversed(list(zip(peers, copies))):
             copy.wait()
             summed = summed + parts_in[turn, d].astype(F32)
@@ -256,7 +254,6 @@
             pltpu.VMEM((rows, wide), F32),
             pltpu.VMEM((8, line, LANES), BF16),
             pltpu.VMEM((8, line, LANES), BF16),
-            pltpu.VMEM((2, n_wide, part, wide), F32),
             pltpu.VMEM((2, n_wide, part, wide), BF16),
             pltpu.VMEM((2, n_wide - 1, part, wide), BF16),
             pltpu.VMEM((part, wide), BF16),

time: 17.1 us -> 17.1 us (level)
  no operation moved by 1% of the time
where the time goes in v7:
time: 17.1 us; the launch traced here: 16.9 us
  Pallas kernels  16.3 us (95%)
  other arithmetic  0.64 us (4%)
    pallas_call x1, Pallas kernels, shards(): pl.pallas_call(functools.partial(kernel, n_wide, n_blk, grid, group), out...  16.3 us
    neg x1, other arithmetic, shards(): return -result  0.64 us

profile of v7, /device:TPU:0, one launch (start us, length us, event | category | flops | bytes accessed | tf_op | source)
XLA Modules:
  0.0 16.9 jit_solution(6539933900046237522)
XLA Ops:
  0.0 16.3 %shard_map.91 = f32[1,8000]{1,0:T(1,128)S(1)} custom-call(bf16[1,64000]{1,0:T(2,128)(2,1)} %src_hbm.1, bf16[1,64000]{1,0:T(2,128)(2,1)} %tgt_hbm.1, bf16[320,320]{1,0:T(8,128)(2,1)} %constant.14.clone.rest_0_, bf16[320,320]{1,0:T(8,128)(2,1)} %constant.15.clone.rest_1_, bf16[200,200]{1,0:T(8,128)(2,1)} %constant.16.clone.rest_2_, ...), custom_call_target="tpu_custom_call" | custom-call | tf_op jit(solution)/shard_map/pallas_call | solution.py:242
  16.3 0.6 %neg.3 = f32[1,8000]{1,0:T(1,128)} negate(f32[1,8000]{1,0:T(1,128)S(1)} %shard_map.91) | non-fusion elementwise | flops 8000 | bytes 64000 | tf_op jit(solution)/shard_map/neg | solution.py:268
